TPU v7x, 128 devices: a whole 4x4x4 slice. The times are simulated.
128 devices in a mesh: grp: 4 (over y), tile: 32 (over z, x, core).
Axes of the slice: x: 4, y: 4, z: 4, core: 2. Of those that a mesh axis runs over, the one named last changes fastest.
Arguments:
- screens: bfloat16 [3, 131072, 256], P(None, ('grp', 'tile')), may hold values from -4 to 4
- interp_weights: bfloat16 [3, 4, 256, 256], replicated, may hold values from -0.375 to 0.375
- footprint: int32 [32768, 3, 4], P(('grp', 'tile')), may hold values from 0 to 131071, as said below
- illumination: float32 [32768, 256], P(('grp', 'tile')), may hold values from 0.3 to 1
- cm_values: bfloat16 [896, 16, 16, 2, 128], P('tile', 'grp'), may hold values from -0.09375 to 0.09375
- cm_columns: int32 [896, 16], P('tile', 'grp'), may hold values from 0 to 255, as said below
- prev_commands: float32 [14336], P('tile'), may hold values from 0 to 5
- owner_map: int32 [14336], P('tile'), may hold values from 0 to 2, as said below
- dm_gain: float32 [3], replicated, may hold values from 0.2 to 1
Outputs:
- slopes: float32 [2, 32768], P(None, ('grp', 'tile'))
- commands: float32 [14336], P('tile')
Inputs may be any that keep to these rules, and one draw needn't show every extreme that they name: `footprint`: the blocks of subaperture s lie among the 1024 blocks of the device holding s and the 256 blocks on either side of them, counted cyclically over all 131072 blocks; some subaperture reaches each end. `cm_columns`: nonzero block n names a column block from (n // 4) * 64 up to that plus 64 - 1. `owner_map`: every mirror owns some actuator.
All inputs are finite; a program needn't handle non-finite values.
Results may differ from a plain program's by a relative error of at most 0.0024.
Values may be sent and summed in bfloat16 or wider, within the bound.
No kernel may reach another device: no remote copies, remote signals or barrier semaphores. Data moves between devices by JAX's collectives and lax.ppermute only.
A program may use at most 64 MiB of HBM per device.

v0:
```python
import math

import jax
import jax.numpy as jnp
import numpy as np
from jax import lax
from jax.experimental import pallas as pl
from jax.experimental.pallas import tpu as pltpu
from jax.sharding import PartitionSpec as P


SIDE = 16
DEVICES = ("grp", "tile")
LANES = 128
EDGE = 256


def swap(block, step):
    count = lax.axis_size(DEVICES)
    route = [(i, (i + step if i % 2 else i - step) % count) for i in range(count)]
    return lax.ppermute(block, DEVICES, route)


def transform_table(side):
    index = np.arange(side * side)
    rows, cols = index // side, index % side
    turns = (rows[:, None] * rows[None, :] + cols[:, None] * cols[None, :]) % side
    angle = turns.astype(np.float32) * np.float32(2.0 * math.pi / side)
    cosine, sine = np.cos(angle), np.sin(angle)
    table = np.concatenate(
        [np.concatenate([cosine, -sine], 1), np.concatenate([sine, cosine], 1)], 0
    )
    return jnp.asarray(table.T.astype(jnp.bfloat16))


def sine_cosine(angle):
    turns = jnp.floor(angle * np.float32(2.0 / math.pi) + 0.5)
    rest = angle - turns * np.float32(1.5703125)
    rest = rest - turns * np.float32(4.837512969970703125e-4)
    rest = rest - turns * np.float32(7.54978995489188216e-8)
    sq = rest * rest
    sine = (np.float32(-1.9515295891e-4) * sq + np.float32(8.3321608736e-3)) * sq
    sine = (sine - np.float32(1.6666654611e-1)) * sq * rest + rest
    cosine = (np.float32(2.443315711809948e-5) * sq - np.float32(1.388731625493765e-3)) * sq
    cosine = (cosine + np.float32(4.166664568298827e-2)) * sq * sq - np.float32(0.5) * sq + 1.0
    quarter = turns.astype(jnp.int32)
    odd = (quarter & 1) == 1
    out_sine = jnp.where(odd, cosine, sine)
    out_cosine = jnp.where(odd, sine, cosine)
    out_sine = jnp.where((quarter & 2) == 2, -out_sine, out_sine)
    out_cosine = jnp.where(((quarter + 1) & 2) == 2, -out_cosine, out_cosine)
    return out_sine, out_cosine


def offsets_of(foot_rows, start, total):
    away = foot_rows - start
    away = jnp.where(away < -(total // 2), away + total, away)
    away = jnp.where(away >= total // 2, away - total, away)
    away = away.astype(jnp.float32)
    foot, subs = away.shape
    filled = jnp.concatenate([away, jnp.zeros((8 - foot, subs), jnp.float32)], 0)
    return filled.T.astype(jnp.int32)


def hits(column, first, count):
    column = jnp.broadcast_to(column, (column.shape[0], LANES)).astype(jnp.int16)
    lane = lax.broadcasted_iota(jnp.int16, column.shape, 1)
    one, zero = jnp.bfloat16(1), jnp.bfloat16(0)
    parts = [
        jnp.where(lane == column - jnp.int16(first + b), one, zero)
        for b in range(0, count, LANES)
    ]
    return jnp.concatenate(parts, 1)


def edges(
    screens_ref, matrix_ref, cols_hbm, owner_hbm, outer_ref, inner_ref, cm_ref, picks_ref, spot_ref,
    cols_ref, owner_ref, sems, *, columns, mirrors
):
    layers, blocks, _ = screens_ref.shape
    last = (blocks // EDGE - 1) * EDGE
    odd = lax.axis_index("tile") % 2
    outer = pl.multiple_of(odd * last, EDGE)
    inner = pl.multiple_of((1 - odd) * last, EDGE)
    copies = []
    for first, ref in ((outer, outer_ref), (inner, inner_ref)):
        for layer in range(layers):
            block = screens_ref.at[layer, pl.ds(first, EDGE)]
            copies.append(pltpu.make_async_copy(block, ref.at[layer], sems.at[len(copies)]))
    copies.append(pltpu.make_async_copy(matrix_ref, cm_ref, sems.at[len(copies)]))
    small = [
        pltpu.make_async_copy(cols_hbm, cols_ref, sems.at[len(copies)]),
        pltpu.make_async_copy(owner_hbm, owner_ref, sems.at[len(copies) + 1]),
    ]
    for copy in small + copies:
        copy.start()
    positions, rowblk = cols_ref.shape
    acts = owner_ref.shape[1]
    rb = acts // rowblk
    act = lax.broadcasted_iota(jnp.int32, (acts, LANES), 0)
    wide = lax.broadcasted_iota(jnp.int32, (acts, LANES), 1)
    over = jnp.where(act % rb == (wide % (2 * rb)) // 2, 1.0, 0.0).astype(jnp.bfloat16)
    for copy in small:
        copy.wait()
    cols = (cols_ref[...] - lax.axis_index("grp") * columns).astype(jnp.float32)
    lane = lax.broadcasted_iota(jnp.int32, (positions, LANES), 1)
    place = lax.broadcasted_iota(jnp.int32, (positions, LANES), 0)
    spread = jnp.where(lane // (2 * rb) == place, 1.0, 0.0)
    cols = lax.dot_general(
        cols, spread, (((0,), (0,)), ((), ())), preferred_element_type=jnp.float32
    ).astype(jnp.int32)
    comp = lax.broadcasted_iota(jnp.int32, cols.shape, 1) % 2
    height = spot_ref.shape[0]
    spot_ref[...] = jnp.concatenate(
        [cols * 2 + comp, jnp.full((height - rowblk, LANES), -1, jnp.int32)], 0
    )
    act = lax.broadcasted_iota(jnp.int32, (rowblk, acts), 1)
    block = lax.broadcasted_iota(jnp.int32, (rowblk, acts), 0)
    held = jnp.where(act // rb == block, owner_ref[...], 0)
    held = held.astype(jnp.float32).astype(jnp.bfloat16)
    owners = jnp.dot(held, over, preferred_element_type=jnp.float32)
    target = cols * (2 * mirrors) + comp * mirrors + owners.astype(jnp.int32)
    row = lax.broadcasted_iota(jnp.int16, (picks_ref.shape[0], LANES), 0)
    one, zero = jnp.bfloat16(1), jnp.bfloat16(0)
    for i in range(rowblk):
        named = jnp.broadcast_to(target[i : i + 1, :], row.shape).astype(jnp.int16)
        picks_ref[:, i * LANES : (i + 1) * LANES] = jnp.where(row == named, one, zero)
    for copy in copies:
        copy.wait()


def mirror_rows(
    gain_ref, owner_ref, prev_ref, picks_ref, cm_ref, sent_ref, state_ref, extra_ref, half_ref, sems
):
    tiles, threes, fours, _ = sent_ref.shape
    mirrors = gain_ref.shape[0]
    acts = owner_ref.shape[1]
    half = tiles // 2
    rows = half * threes * fours
    copies = []
    for part in range(2):
        sums = jnp.dot(
            picks_ref[part * rows : (part + 1) * rows, :],
            cm_ref[...],
            preferred_element_type=jnp.float32,
        )
        for t in range(half):
            for j in range(threes):
                at = (t * threes + j) * fours
                half_ref[part * half + t, j] = sums[at : at + fours]
        span = pl.ds(part * half, half)
        copies.append(
            pltpu.make_async_copy(half_ref.at[span], sent_ref.at[span], sems.at[part])
        )
        copies[part].start()
    owner = owner_ref[...]
    lane = lax.broadcasted_iota(jnp.int32, (1, LANES), 1)
    extra = jnp.zeros((1, LANES), jnp.float32)
    gain = jnp.zeros(owner.shape, jnp.float32)
    for m in range(mirrors):
        mine = owner == m
        gain = jnp.where(mine, gain_ref[m], gain)
        prev = jnp.sum(jnp.where(mine, prev_ref[...], 0.0), axis=1, keepdims=True)
        number = jnp.sum(jnp.where(mine, 1.0, 0.0), axis=1, keepdims=True)
        extra = jnp.where(lane == mirrors + m, prev, extra)
        extra = jnp.where(lane == 2 * mirrors + m, number, extra)
    extra_ref[...] = extra
    lines = state_ref.shape[0] // 3
    missing = lines * LANES - acts
    rows = []
    for values, fill in ((owner.astype(jnp.float32), -1.0), (prev_ref[...], 0.0), (gain, 0.0)):
        values = jnp.concatenate([values, jnp.full((1, missing), fill, jnp.float32)], 1)
        rows += [values[:, i * LANES : (i + 1) * LANES] for i in range(lines)]
    state_ref[...] = jnp.concatenate(rows, 0)
    for copy in copies:
        copy.wait()


def pick_own(foot_ref, screens_ref, inner_ref, picked_ref, *, total):
    layers, foot, _ = foot_ref.shape
    blocks, pixels = screens_ref.shape[1:]
    start = lax.axis_index(DEVICES) * blocks
    first = (1 - lax.axis_index("tile") % 2) * (blocks + EDGE) - EDGE
    for layer in range(layers):
        offsets = offsets_of(foot_ref[layer], start, total)
        for k in range(foot):
            column = offsets[:, k : k + 1]
            rows = jnp.dot(
                hits(column, 0, blocks), screens_ref[layer], preferred_element_type=jnp.float32
            )
            rows = rows + jnp.dot(
                hits(column - first, 0, EDGE),
                inner_ref[layer],
                preferred_element_type=jnp.float32,
            )
            picked_ref[layer, :, k * pixels : (k + 1) * pixels] = rows.astype(jnp.bfloat16)


def sense_rest(
    foot_ref, outer_ref, weights_ref, own_ref, illum_ref, table_ref, slopes_ref, words_ref, *,
    total, blocks
):
    layers, foot, subs = foot_ref.shape
    pixels = illum_ref.shape[1]
    start = lax.axis_index(DEVICES) * blocks
    first = (lax.axis_index("tile") % 2) * (blocks + EDGE) - EDGE
    phase = None
    for layer in range(layers):
        offsets = offsets_of(foot_ref[layer], start, total)
        for k in range(foot):
            found = hits(offsets[:, k : k + 1] - first, 0, EDGE)
            rows = jnp.dot(found, outer_ref[layer], preferred_element_type=jnp.float32)
            rows = rows.astype(jnp.bfloat16) + own_ref[layer, :, k * pixels : (k + 1) * pixels]
            part = jnp.dot(rows, weights_ref[layer, k], preferred_element_type=jnp.float32)
            phase = part if phase is None else phase + part
    phase = phase.T
    illum = illum_ref[...].T
    sine, cosine = sine_cosine(phase)
    field = jnp.concatenate([illum * cosine, illum * sine], 0).astype(jnp.bfloat16)
    spectrum = jnp.dot(table_ref[...], field, preferred_element_type=jnp.float32)
    real_part = spectrum[:pixels]
    imag_part = spectrum[pixels:]
    intensity = real_part * real_part + imag_part * imag_part
    row = lax.broadcasted_iota(jnp.int32, intensity.shape, 0)
    cv = row % SIDE
    cu = row // SIDE
    cv = (cv - SIDE * (cv >= SIDE // 2).astype(jnp.int32)).astype(jnp.float32)
    cu = (cu - SIDE * (cu >= SIDE // 2).astype(jnp.int32)).astype(jnp.float32)
    whole = jnp.sum(intensity, axis=0, keepdims=True)
    slope_x = jnp.sum(intensity * cv, axis=0, keepdims=True) / whole
    slope_y = jnp.sum(intensity * cu, axis=0, keepdims=True) / whole
    slopes = jnp.concatenate([slope_x, slope_y], 0)
    slopes_ref[...] = slopes
    words = slopes.astype(jnp.bfloat16).astype(jnp.float32)
    words = [words[:, h * LANES : (h + 1) * LANES] for h in range(subs // LANES)]
    words_ref[...] = jnp.concatenate(words, 0)


def pack(words_ref, rows_ref, extra_ref, sent_ref, *, mirrors):
    words = words_ref[...]
    sums = jnp.sum(rows_ref[...], axis=0)
    lane = lax.broadcasted_iota(jnp.int32, (1, LANES), 1)
    line = extra_ref[...]
    for m in range(mirrors):
        product = jnp.zeros((1, LANES), jnp.float32)
        for k in range(words.shape[0]):
            at = k * mirrors + m
            row = sums[at // sums.shape[1], at % sums.shape[1]][None]
            product = product + row * words[k : k + 1]
        line = jnp.where(lane == m, jnp.sum(product, axis=1, keepdims=True), line)
    high = line.astype(jnp.bfloat16).astype(jnp.float32)
    middle = (line - high).astype(jnp.bfloat16).astype(jnp.float32)
    low = line - high - middle
    rows = jnp.concatenate([words, high, middle, low, jnp.zeros_like(low)], 0)
    sent_ref[...] = jnp.broadcast_to(rows.astype(jnp.bfloat16)[None], sent_ref.shape)


def reconstruct(words_ref, cm_ref, spot_ref, sent_ref, *, rb):
    got = words_ref[...].astype(jnp.float32)
    words = got[:, :4, :].reshape(-1, LANES).astype(jnp.bfloat16)
    line = jnp.sum(got, axis=0)
    line = line[4:5] + line[5:6] + line[6:7]
    rowblk = cm_ref.shape[0] // LANES
    row = lax.broadcasted_iota(jnp.int32, (words.shape[0], LANES), 0)
    parts = []
    step = math.gcd(rowblk, 4)
    for first in range(0, rowblk, step):
        product = lax.dot_general(
            words,
            cm_ref[first * LANES : (first + step) * LANES, :],
            (((1,), (1,)), ((), ())),
            preferred_element_type=jnp.float32,
        )
        for i in range(step):
            spot = spot_ref[first + i : first + i + 1, :]
            chosen = jnp.where(row == spot, product[:, i * LANES : (i + 1) * LANES], 0.0)
            parts.append(jnp.sum(chosen, axis=0, keepdims=True))
    height = spot_ref.shape[0]
    if height > rowblk:
        parts.append(jnp.zeros((height - rowblk, LANES), jnp.float32))
    parts = jnp.concatenate(parts, 0)
    source = lax.broadcasted_iota(jnp.int32, (LANES, LANES), 0)
    lane = lax.broadcasted_iota(jnp.int32, (LANES, LANES), 1)
    fold = jnp.where((source % (2 * rb)) // 2 == lane % rb, 1.0, 0.0)
    spread = jnp.dot(
        parts, fold, preferred_element_type=jnp.float32, precision=lax.Precision.HIGHEST
    )
    per = LANES // rb
    block = lax.broadcasted_iota(jnp.int32, spread.shape, 0)
    lane = lax.broadcasted_iota(jnp.int32, spread.shape, 1)
    spread = jnp.where(lane // rb == block % per, spread, 0.0)
    recon = jnp.sum(spread.reshape(height // per, per, LANES), axis=1)
    rest = sent_ref.shape[0] - recon.shape[0] - 1
    sent_ref[...] = jnp.concatenate([recon, line, jnp.zeros((rest, LANES), jnp.float32)], 0)


def settle(*refs, mirrors):
    *got_refs, state_ref, found_ref, slopes_ref, commands_ref = refs
    slopes_ref[...] = found_ref[...]
    lines = state_ref.shape[0] // 3
    sums = got_refs[0][...]
    for got_ref in got_refs[1:]:
        sums = sums + got_ref[...]
    line = sums[lines : lines + 1]
    share = 1.0 / len(got_refs)
    lane = lax.broadcasted_iota(jnp.int32, line.shape, 1)

    def entry(at):
        return jnp.sum(jnp.where(lane == at, line, 0.0), axis=1, keepdims=True)

    owner = state_ref[:lines]
    gain = state_ref[2 * lines :]
    piston = jnp.zeros(owner.shape, jnp.float32)
    for m in range(mirrors):
        total = share * entry(mirrors + m) - gain * entry(m)
        count = share * entry(2 * mirrors + m)
        piston = jnp.where(owner == float(m), total / count, piston)
    commands = state_ref[lines : 2 * lines] - gain * sums[:lines] - piston
    acts = commands_ref.shape[0]
    for i in range(lines):
        some = min(LANES, acts - i * LANES)
        commands_ref[i * LANES : i * LANES + some] = commands[i, :some]


def on_device(
    screens,
    interp_weights,
    footprint,
    illumination,
    cm_values,
    cm_columns,
    prev_commands,
    owner_map,
    dm_gain,
):
    layers, blk_dev, pixels = screens.shape
    subs, _, foot = footprint.shape
    groups, tiles = lax.axis_size("grp"), lax.axis_size("tile")
    total = blk_dev * groups * tiles
    rowblk, positions, rb, comps, cbs = cm_values.shape
    acts = rowblk * rb
    mirrors = dm_gain.shape[0]
    height = -(-acts // LANES) * LANES // rb
    lines = height * rb // LANES
    smem = pl.BlockSpec(memory_space=pltpu.SMEM)
    vmem = pl.BlockSpec(memory_space=pltpu.VMEM)
    limit = pltpu.CompilerParams(vmem_limit_bytes=24 * 2**20)
    tight = pltpu.CompilerParams(vmem_limit_bytes=24 * 2**20)
    f32 = jnp.float32

    edge = jax.ShapeDtypeStruct((layers, EDGE, pixels), screens.dtype)
    hbm = pl.BlockSpec(memory_space=pltpu.HBM)
    cm = cm_values.reshape(rowblk * positions * rb * comps, cbs)
    held = owner_map.reshape(1, acts)
    sums = 4 * mirrors

    def stay(array):
        return pltpu.with_memory_space_constraint(array, pltpu.HBM)

    outer, inner, loaded, picks, spot = pl.pallas_call(
        lambda *refs: edges(*refs, columns=tiles * subs // cbs, mirrors=mirrors),
        in_specs=[hbm] * 4,
        out_specs=[vmem] * 5,
        out_shape=[
            edge,
            edge,
            jax.ShapeDtypeStruct(cm.shape, cm.dtype),
            jax.ShapeDtypeStruct((tiles * sums, cm.shape[0]), jnp.bfloat16),
            jax.ShapeDtypeStruct((height, LANES), jnp.int32),
        ],
        scratch_shapes=[
            pltpu.VMEM((positions, rowblk), jnp.int32),
            pltpu.VMEM((1, acts), jnp.int32),
            pltpu.SemaphoreType.DMA((2 * layers + 3,)),
        ],
        compiler_params=limit,
        name="edges",
    )(stay(screens), stay(cm), stay(cm_columns.T), stay(held))
    outer = swap(outer, 1)
    inner = swap(inner, -1)

    rows, state, extra = pl.pallas_call(
        mirror_rows,
        in_specs=[smem] + [vmem] * 4,
        out_specs=[hbm, vmem, vmem],
        out_shape=(
            jax.ShapeDtypeStruct((tiles, sums // 4, 4, LANES), f32),
            jax.ShapeDtypeStruct((3 * lines, LANES), f32),
            jax.ShapeDtypeStruct((1, LANES), f32),
        ),
        scratch_shapes=[
            pltpu.VMEM((tiles, sums // 4, 4, LANES), f32),
            pltpu.SemaphoreType.DMA((2,)),
        ],
        compiler_params=tight,
        name="mirror_rows",
    )(dm_gain, held, prev_commands.reshape(1, acts), picks, loaded)
    foot_rows = jnp.transpose(footprint, (1, 2, 0))
    rows, foot_rows = lax.optimization_barrier((rows, foot_rows))
    rows = lax.all_to_all(rows, "tile", 0, 0)

    picked = pl.pallas_call(
        lambda *refs: pick_own(*refs, total=total),
        in_specs=[vmem] * 3,
        out_shape=jax.ShapeDtypeStruct((layers, subs, foot * pixels), screens.dtype),
        compiler_params=tight,
        name="pick_own",
    )(foot_rows, screens, inner)
    slopes, words = pl.pallas_call(
        lambda *refs: sense_rest(*refs, total=total, blocks=blk_dev),
        in_specs=[vmem] * 6,
        out_shape=(
            jax.ShapeDtypeStruct((2, subs), f32),
            jax.ShapeDtypeStruct((2 * subs // LANES, LANES), f32),
        ),
        compiler_params=limit,
        name="sense_rest",
    )(
        foot_rows, outer, interp_weights, picked, illumination, transform_table(SIDE)
    )
    packed = pl.pallas_call(
        lambda *refs: pack(*refs, mirrors=mirrors),
        in_specs=[vmem] * 3,
        out_shape=jax.ShapeDtypeStruct((tiles, 8, LANES), jnp.bfloat16),
        compiler_params=limit,
        name="pack",
    )(words, rows, extra)

    gathered = lax.all_to_all(packed, "tile", 0, 0)
    sent = pl.pallas_call(
        lambda *refs: reconstruct(*refs, rb=rb),
        in_specs=[vmem] * 3,
        out_shape=jax.ShapeDtypeStruct((8, LANES), f32),
        compiler_params=limit,
        name="reconstruct",
    )(gathered, cm, spot)
    got = [sent]
    for far in range(1, groups):
        route = [(g, (g + far) % groups) for g in range(groups)]
        got.append(lax.ppermute(sent, "grp", route))
    return pl.pallas_call(
        lambda *refs: settle(*refs, mirrors=mirrors),
        in_specs=[vmem] * (groups + 2),
        out_shape=(
            jax.ShapeDtypeStruct((2, subs), f32),
            jax.ShapeDtypeStruct((acts,), f32),
        ),
        compiler_params=limit,
        name="settle",
    )(*got, state, slopes)


def solution(mesh):
    in_specs = (
        P(None, ("grp", "tile"), None),
        P(),
        P(("grp", "tile"), None, None),
        P(("grp", "tile"), None),
        P("tile", "grp", None, None, None),
        P("tile", "grp"),
        P("tile"),
        P("tile"),
        P(),
    )
    out_specs = (P(None, ("grp", "tile")), P("tile"))
    return jax.shard_map(
        on_device, mesh=mesh, in_specs=in_specs, out_specs=out_specs, check_vma=False
    )
```

profile of v0, /device:TPU:1, one launch (start us, length us, event | category | flops | bytes accessed | tf_op | source)
XLA Modules:
  0.0 44.3 jit_solution(3459643588302291205)
XLA Ops:
  0.7 1.6 %edges.1 = (bf16[3,256,256]{2,1,0:T(8,128)(2,1)S(1)}, bf16[3,256,256]{2,1,0:T(8,128)(2,1)S(1)}, bf16[3584,128]{1,0:T(8,128)(2,1)S(1)}, bf16[384,3584]{1,0:T(8,128)(2,1)S(1)}, s32[32,128]{1,0:T(8,128)S(1)}) custom-call(bf16[3,1024,256]{2,1,0:T(8,128)(2,1)} %refs_1_.1, bf16[3584,128]{1,0:T(8,128)(2,1)} %bitcast.5, s32[4,28]{1,0:T(4,128)} %bitcast.12, ...), custom_call_target="tpu_custom_call" | custom-call | tf_op jit(solution)/shard_map/edges/pallas_call | solution.py:360
  2.3 1.5 %collective-permute-start.1 = (bf16[3,256,256]{2,1,0:T(8,128)(2,1)S(1)}, bf16[3,256,256]{2,1,0:T(8,128)(2,1)S(1)}, u32[]{:S(2)}, u32[]{:S(2)}) collective-permute-start(bf16[3,256,256]{2,1,0:T(8,128)(2,1)S(1)} %get-tuple-element.19), channel_id=1, source_target_pairs={{0,1},{1,0},{2,3},{3,2},{4,5},{5,4},{6,7},{7,6},{8,9},{9,8},{10,11... | collective-permute-start | bytes 1179656 | tf_op jit(solution)/shard_map/ppermute | solution.py:21
  3.8 1.3 %collective-permute-start = (bf16[3,256,256]{2,1,0:T(8,128)(2,1)S(1)}, bf16[3,256,256]{2,1,0:T(8,128)(2,1)S(1)}, u32[]{:S(2)}, u32[]{:S(2)}) collective-permute-start(bf16[3,256,256]{2,1,0:T(8,128)(2,1)S(1)} %get-tuple-element.18), channel_id=1, source_target_pairs={{0,127},{1,2},{2,1},{3,4},{4,3},{5,6},{6,5},{7,8},{8,7},{9,10},{10... | collective-permute-start | bytes 1179656 | tf_op jit(solution)/shard_map/ppermute | solution.py:21
  5.1 0.0 copy-start.5
  5.1 2.1 %mirror_rows.1 = (f32[32,3,4,128]{3,2,1,0:T(4,128)}, f32[12,128]{1,0:T(8,128)S(1)}, f32[1,128]{1,0:T(1,128)S(1)}) custom-call(f32[3]{0:T(128)S(1)} %copy-done.8, s32[1,448]{1,0:T(1,128)S(1)} %bitcast.10, f32[1,448]{1,0:T(1,128)S(1)} %bitcast.11, bf16[384,3584]{1,0:T(8,128)(2,1)S(1)} %get-tuple-element.14.picks_ref, ...), custom_call_target="tpu_custom_call" | custom-call | tf_op jit(solution)/shard_map/mirror_rows/pallas_call | solution.py:382
  7.2 11.1 %all-to-all-start = ((f32[32,3,4,128]{3,2,1,0:T(4,128)}), f32[32,3,4,128]{3,2,1,0:T(4,128)S(1)}, u32[]{:S(2)}, u32[]{:S(2)}) async-start(f32[32,3,4,128]{3,2,1,0:T(4,128)} %get-tuple-element.21), calls=%async_computation | async-start | bytes 393216 | tf_op jit(solution)/shard_map/all_to_all | solution.py:400
  18.3 0.0 copy-start.2
  18.3 0.0 copy-start.3
  18.3 0.0 copy-start.4
  18.4 0.0 collective-permute-done.1.refs_2_
  18.4 2.5 %pick_own.1.refs_3_ = bf16[3,256,1024]{2,1,0:T(8,128)(2,1)S(1)} custom-call(s32[3,4,256]{2,1,0:T(4,128)S(1)} %bitcast.7, bf16[3,1024,256]{2,1,0:T(8,128)(2,1)S(1)} %copy-done, bf16[3,256,256]{2,1,0:T(8,128)(2,1)S(1)} %collective-permute-done.1.refs_2_), custom_call_target="tpu_custom_call" | custom-call | tf_op jit(solution)/shard_map/pick_own/pallas_call | solution.py:402
  20.9 0.0 copy-start.1
  21.0 2.3 %sense_rest.1 = (f32[2,256]{1,0:T(2,128)S(1)}, f32[4,128]{1,0:T(4,128)S(1)}) custom-call(s32[3,4,256]{2,1,0:T(4,128)S(1)} %bitcast.8, bf16[3,256,256]{2,1,0:T(8,128)(2,1)S(1)} %collective-permute-done.refs_1_, bf16[3,4,256,256]{3,2,1,0:T(8,128)(2,1)S(1)} %copy-done.2, bf16[3,256,1024]{2,1,0:T(8,128)(2,1)S(1)} %pick_own.1.refs_3_, f32[256,256]{1,0:T(8,128)S(1)} %copy-done.4, ...), custom_call_target="tpu_custom_call" | custom-call | tf_op jit(solution)/shard_map/sense_rest/pallas_call | solution.py:409
  23.3 3.4 %all-to-all-done.refs_1_ = f32[32,3,4,128]{3,2,1,0:T(4,128)S(1)} async-done(((f32[32,3,4,128]{3,2,1,0:T(4,128)}), f32[32,3,4,128]{3,2,1,0:T(4,128)S(1)}, u32[]{:S(2)}, u32[]{:S(2)}) %all-to-all-start) | async-done | bytes 196640 | tf_op jit(solution)/shard_map/all_to_all | solution.py:400
  26.7 0.1 pack.1
  26.8 11.3 %all_to_all.10.refs_0_ = bf16[32,8,128]{2,1,0:T(8,128)(2,1)S(1)} all-to-all(bf16[32,8,128]{2,1,0:T(8,128)(2,1)S(1)} %pack.1), channel_id=1, replica_groups=mesh['grp'=4,'tile'=32] {'tile'}, dimensions={0} | all-to-all | bytes 131072 | tf_op jit(solution)/shard_map/all_to_all | solution.py:429
  38.1 0.6 %reconstruct.1.refs_0_ = f32[8,128]{1,0:T(8,128)S(1)} custom-call(bf16[32,8,128]{2,1,0:T(8,128)(2,1)S(1)} %all_to_all.10.refs_0_, bf16[3584,128]{1,0:T(8,128)(2,1)S(1)} %bitcast.6, s32[32,128]{1,0:T(8,128)S(1)} %get-tuple-element.23.refs_2_), custom_call_target="tpu_custom_call" | custom-call | tf_op jit(solution)/shard_map/reconstruct/pallas_call | solution.py:430
  38.7 0.5 %collective-permute-start.4 = (f32[8,128]{1,0:T(8,128)S(1)}, f32[8,128]{1,0:T(8,128)S(1)}, u32[]{:S(2)}, u32[]{:S(2)}) collective-permute-start(f32[8,128]{1,0:T(8,128)S(1)} %reconstruct.1.refs_0_), channel_id=1, source_target_pairs={{0,96},{32,0},{64,32},{96,64},{1,97},{33,1},{65,33},{97,65},{2,98}... | collective-permute-start | bytes 12296 | tf_op jit(solution)/shard_map/ppermute | solution.py:440
  39.2 0.1 collective-permute-start.3
  39.3 1.0 %collective-permute-start.2 = (f32[8,128]{1,0:T(8,128)S(1)}, f32[8,128]{1,0:T(8,128)S(1)}, u32[]{:S(2)}, u32[]{:S(2)}) collective-permute-start(f32[8,128]{1,0:T(8,128)S(1)} %reconstruct.1.refs_0_), channel_id=1, source_target_pairs={{0,32},{32,64},{64,96},{96,0},{1,33},{33,65},{65,97},{97,1},{2,34}... | collective-permute-start | bytes 12296 | tf_op jit(solution)/shard_map/ppermute | solution.py:440
  40.3 1.0 %collective-permute-done.4.refs_3_ = f32[8,128]{1,0:T(8,128)S(1)} collective-permute-done((f32[8,128]{1,0:T(8,128)S(1)}, f32[8,128]{1,0:T(8,128)S(1)}, u32[]{:S(2)}, u32[]{:S(2)}) %collective-permute-start.4) | collective-permute-done | bytes 4128 | tf_op jit(solution)/shard_map/ppermute | solution.py:440
  41.2 2.0 %collective-permute-done.3.refs_2_ = f32[8,128]{1,0:T(8,128)S(1)} collective-permute-done((f32[8,128]{1,0:T(8,128)S(1)}, f32[8,128]{1,0:T(8,128)S(1)}, u32[]{:S(2)}, u32[]{:S(2)}) %collective-permute-start.3) | collective-permute-done | bytes 4128 | tf_op jit(solution)/shard_map/ppermute | solution.py:440
  43.2 0.4 collective-permute-done.2.refs_1_
  43.6 0.7 %settle.1 = (f32[2,256]{1,0:T(2,128)}, f32[448]{0:T(512)}) custom-call(f32[8,128]{1,0:T(8,128)S(1)} %reconstruct.1.refs_0_, f32[8,128]{1,0:T(8,128)S(1)} %collective-permute-done.2.refs_1_, f32[8,128]{1,0:T(8,128)S(1)} %collective-permute-done.3.refs_2_, f32[8,128]{1,0:T(8,128)S(1)} %collective-permute-done.4.refs_3_, ...), custom_call_target="tpu_custom_call" | custom-call | tf_op jit(solution)/shard_map/settle/pallas_call | solution.py:441
  (14 shorter events, 0.0 us)
Async XLA Ops:
  0.6 4.4 %copy-start.6 = (s32[448]{0:T(512)S(1)}, s32[448]{0:T(512)}, u32[]{:S(2)}) copy-start(s32[448]{0:T(512)} %param.17) | copy-start | bytes 5380
  0.6 4.4 %copy-start.8 = (f32[3]{0:T(128)S(1)}, f32[3]{0:T(128)}, u32[]{:S(2)}) copy-start(f32[3]{0:T(128)} %gain_ref.1) | copy-start | bytes 40
  0.7 4.4 %copy-start.7 = (f32[448]{0:T(512)S(1)}, f32[448]{0:T(512)}, u32[]{:S(2)}) copy-start(f32[448]{0:T(512)} %param.16) | copy-start | bytes 5380
  2.3 16.0 %collective-permute-start.1 = (bf16[3,256,256]{2,1,0:T(8,128)(2,1)S(1)}, bf16[3,256,256]{2,1,0:T(8,128)(2,1)S(1)}, u32[]{:S(2)}, u32[]{:S(2)}) collective-permute-start(bf16[3,256,256]{2,1,0:T(8,128)(2,1)S(1)} %get-tuple-element.19), channel_id=1, source_target_pairs={{0,1},{1,0},{2,3},{3,2},{4,5},{5,4},{6,7},{7,6},{8,9},{9,8},{10,11... | collective-permute-start | bytes 1179656 | tf_op jit(solution)/shard_map/ppermute | solution.py:21
  3.8 17.2 %collective-permute-start = (bf16[3,256,256]{2,1,0:T(8,128)(2,1)S(1)}, bf16[3,256,256]{2,1,0:T(8,128)(2,1)S(1)}, u32[]{:S(2)}, u32[]{:S(2)}) collective-permute-start(bf16[3,256,256]{2,1,0:T(8,128)(2,1)S(1)} %get-tuple-element.18), channel_id=1, source_target_pairs={{0,127},{1,2},{2,1},{3,4},{4,3},{5,6},{6,5},{7,8},{8,7},{9,10},{10... | collective-permute-start | bytes 1179656 | tf_op jit(solution)/shard_map/ppermute | solution.py:21
  5.1 13.3 %copy-start = (bf16[3,1024,256]{2,1,0:T(8,128)(2,1)S(1)}, bf16[3,1024,256]{2,1,0:T(8,128)(2,1)}, u32[]{:S(2)}) copy-start(bf16[3,1024,256]{2,1,0:T(8,128)(2,1)} %refs_1_.1) | copy-start | bytes 4718596
  5.1 13.3 %copy-start.5 = (s32[256,3,4]{0,2,1:T(4,128)S(1)}, s32[256,3,4]{0,2,1:T(4,128)}, u32[]{:S(2)}) copy-start(s32[256,3,4]{0,2,1:T(4,128)} %param.12) | copy-start | bytes 36868
  7.2 19.5 %all-to-all-start = ((f32[32,3,4,128]{3,2,1,0:T(4,128)}), f32[32,3,4,128]{3,2,1,0:T(4,128)S(1)}, u32[]{:S(2)}, u32[]{:S(2)}) async-start(f32[32,3,4,128]{3,2,1,0:T(4,128)} %get-tuple-element.21), calls=%async_computation | async-start | bytes 393216 | tf_op jit(solution)/shard_map/all_to_all | solution.py:400
  18.3 2.6 %copy-start.2 = (bf16[3,4,256,256]{3,2,1,0:T(8,128)(2,1)S(1)}, bf16[3,4,256,256]{3,2,1,0:T(8,128)(2,1)}, u32[]{:S(2)}) copy-start(bf16[3,4,256,256]{3,2,1,0:T(8,128)(2,1)} %refs_2_.1) | copy-start | bytes 4718596
  18.3 2.6 %copy-start.3 = (bf16[512,512]{1,0:T(8,128)(2,1)S(1)}, bf16[512,512]{1,0:T(8,128)(2,1)}, u32[]{:S(2)}) copy-start(bf16[512,512]{1,0:T(8,128)(2,1)} %constant.2.clone.refs_5_) | copy-start | bytes 1572868
  18.3 2.6 %copy-start.4 = (f32[256,256]{1,0:T(8,128)S(1)}, f32[256,256]{1,0:T(8,128)}, u32[]{:S(2)}) copy-start(f32[256,256]{1,0:T(8,128)} %refs_4_.1) | copy-start | bytes 786436
  20.9 17.1 %copy-start.1 = (bf16[28,4,16,2,128]{4,3,2,1,0:T(2,128)(2,1)S(1)}, bf16[28,4,16,2,128]{4,3,2,1,0:T(2,128)(2,1)}, u32[]{:S(2)}) copy-start(bf16[28,4,16,2,128]{4,3,2,1,0:T(2,128)(2,1)} %param.14) | copy-start | bytes 2752516
  38.7 2.5 %collective-permute-start.4 = (f32[8,128]{1,0:T(8,128)S(1)}, f32[8,128]{1,0:T(8,128)S(1)}, u32[]{:S(2)}, u32[]{:S(2)}) collective-permute-start(f32[8,128]{1,0:T(8,128)S(1)} %reconstruct.1.refs_0_), channel_id=1, source_target_pairs={{0,96},{32,0},{64,32},{96,64},{1,97},{33,1},{65,33},{97,65},{2,98}... | collective-permute-start | bytes 12296 | tf_op jit(solution)/shard_map/ppermute | solution.py:440
  39.2 4.0 %collective-permute-start.3 = (f32[8,128]{1,0:T(8,128)S(1)}, f32[8,128]{1,0:T(8,128)S(1)}, u32[]{:S(2)}, u32[]{:S(2)}) collective-permute-start(f32[8,128]{1,0:T(8,128)S(1)} %reconstruct.1.refs_0_), channel_id=1, source_target_pairs={{0,64},{32,96},{64,0},{96,32},{1,65},{33,97},{65,1},{97,33},{2,66}... | collective-permute-start | bytes 12296 | tf_op jit(solution)/shard_map/ppermute | solution.py:440
  39.3 4.3 %collective-permute-start.2 = (f32[8,128]{1,0:T(8,128)S(1)}, f32[8,128]{1,0:T(8,128)S(1)}, u32[]{:S(2)}, u32[]{:S(2)}) collective-permute-start(f32[8,128]{1,0:T(8,128)S(1)} %reconstruct.1.refs_0_), channel_id=1, source_target_pairs={{0,32},{32,64},{64,96},{96,0},{1,33},{33,65},{65,97},{97,1},{2,34}... | collective-permute-start | bytes 12296 | tf_op jit(solution)/shard_map/ppermute | solution.py:440
where the time goes:
time: 45 us; the launch traced here: 44.3 us
  starting transfers between devices  15.4 us (34%)
  blocking collectives  11.3 us (25%)
  Pallas kernels  10 us (22%)
  waiting for transfers between devices  6.76 us (15%)
  between operations  0.81 us (2%)
    all_to_all x1, blocking collectives, on_device(): gathered = lax.all_to_all(packed, 'tile', 0, 0)  11.3 us
    all_to_all x1, starting transfers between devices, on_device(): rows = lax.all_to_all(rows, 'tile', 0, 0)  11.1 us
    ppermute x3, waiting for transfers between devices, on_device(): got.append(lax.ppermute(sent, 'grp', route))  3.38 us
    all_to_all x1, waiting for transfers between devices, on_device(): rows = lax.all_to_all(rows, 'tile', 0, 0)  3.37 us
    ppermute x2, starting transfers between devices, swap(): return lax.ppermute(block, DEVICES, route)  2.76 us
    pallas_call x1, Pallas kernels, on_device(): pl.pallas_call(lambda *refs: pick_own(*refs, total=total), in_specs=[vmem...  2.54 us
    pallas_call x1, Pallas kernels, on_device(): pl.pallas_call(lambda *refs: sense_rest(*refs, total=total, blocks=blk_de...  2.31 us
    pallas_call x1, Pallas kernels, on_device(): pl.pallas_call(mirror_rows, in_specs=[smem] + [vmem] * 4, out_specs=[hbm,...  2.07 us
  transfers between devices with their start and end apart: 6, of which 4 were waited for; matrix products, arithmetic and copies ran while one was open for 0% of the time, Pallas kernels for 16%

commit v1 on v0

--- a/solution.py
+++ b/solution.py
@@ -373,7 +373,7 @@
             pltpu.VMEM((1, acts), jnp.int32),
             pltpu.SemaphoreType.DMA((2 * layers + 3,)),
         ],
-        compiler_params=limit,
+        compiler_params=tight,
         name="edges",
     )(stay(screens), stay(cm), stay(cm_columns.T), stay(held))
     outer = swap(outer, 1)
@@ -413,7 +413,7 @@
             jax.ShapeDtypeStruct((2, subs), f32),
             jax.ShapeDtypeStruct((2 * subs // LANES, LANES), f32),
         ),
-        compiler_params=limit,
+        compiler_params=tight,
         name="sense_rest",
     )(
         foot_rows, outer, interp_weights, picked, illumination, transform_table(SIDE)
@@ -422,7 +422,7 @@
         lambda *refs: pack(*refs, mirrors=mirrors),
         in_specs=[vmem] * 3,
         out_shape=jax.ShapeDtypeStruct((tiles, 8, LANES), jnp.bfloat16),
-        compiler_params=limit,
+        compiler_params=tight,
         name="pack",
     )(words, rows, extra)
 
@@ -431,7 +431,7 @@
         lambda *refs: reconstruct(*refs, rb=rb),
         in_specs=[vmem] * 3,
         out_shape=jax.ShapeDtypeStruct((8, LANES), f32),
-        compiler_params=limit,
+        compiler_params=tight,
         name="reconstruct",
     )(gathered, cm, spot)
     got = [sent]
@@ -445,7 +445,7 @@
             jax.ShapeDtypeStruct((2, subs), f32),
             jax.ShapeDtypeStruct((acts,), f32),
         ),
-        compiler_params=limit,
+        compiler_params=tight,
         name="settle",
     )(*got, state, slopes)
 

time: 45 us -> 45 us (level)
  no operation moved by 1% of the time
where the time goes in v1:
time: 45 us; the launch traced here: 44.3 us
  starting transfers between devices  15.4 us (34%)
  blocking collectives  11.3 us (25%)
  Pallas kernels  10 us (22%)
  waiting for transfers between devices  6.76 us (15%)
  between operations  0.81 us (2%)
    all_to_all x1, blocking collectives, on_device(): gathered = lax.all_to_all(packed, 'tile', 0, 0)  11.3 us
    all_to_all x1, starting transfers between devices, on_device(): rows = lax.all_to_all(rows, 'tile', 0, 0)  11.1 us
    ppermute x3, waiting for transfers between devices, on_device(): got.append(lax.ppermute(sent, 'grp', route))  3.38 us
    all_to_all x1, waiting for transfers between devices, on_device(): rows = lax.all_to_all(rows, 'tile', 0, 0)  3.37 us
    ppermute x2, starting transfers between devices, swap(): return lax.ppermute(block, DEVICES, route)  2.76 us
    pallas_call x1, Pallas kernels, on_device(): pl.pallas_call(lambda *refs: pick_own(*refs, total=total), in_specs=[vmem...  2.54 us
    pallas_call x1, Pallas kernels, on_device(): pl.pallas_call(lambda *refs: sense_rest(*refs, total=total, blocks=blk_de...  2.31 us
    pallas_call x1, Pallas kernels, on_device(): pl.pallas_call(mirror_rows, in_specs=[smem] + [vmem] * 4, out_specs=[hbm,...  2.07 us
  transfers between devices with their start and end apart: 6, of which 4 were waited for; matrix products, arithmetic and copies ran while one was open for 0% of the time, Pallas kernels for 16%

profile of v1, /device:TPU:1, one launch (start us, length us, event | category | flops | bytes accessed | tf_op | source)
XLA Modules:
  0.0 44.3 jit_solution(3459643588302291205)
XLA Ops:
  0.7 1.6 %edges.1 = (bf16[3,256,256]{2,1,0:T(8,128)(2,1)S(1)}, bf16[3,256,256]{2,1,0:T(8,128)(2,1)S(1)}, bf16[3584,128]{1,0:T(8,128)(2,1)S(1)}, bf16[384,3584]{1,0:T(8,128)(2,1)S(1)}, s32[32,128]{1,0:T(8,128)S(1)}) custom-call(bf16[3,1024,256]{2,1,0:T(8,128)(2,1)} %refs_1_.1, bf16[3584,128]{1,0:T(8,128)(2,1)} %bitcast.5, s32[4,28]{1,0:T(4,128)} %bitcast.12, ...), custom_call_target="tpu_custom_call" | custom-call | tf_op jit(solution)/shard_map/edges/pallas_call | solution.py:360
  2.3 1.5 %collective-permute-start.1 = (bf16[3,256,256]{2,1,0:T(8,128)(2,1)S(1)}, bf16[3,256,256]{2,1,0:T(8,128)(2,1)S(1)}, u32[]{:S(2)}, u32[]{:S(2)}) collective-permute-start(bf16[3,256,256]{2,1,0:T(8,128)(2,1)S(1)} %get-tuple-element.19), channel_id=1, source_target_pairs={{0,1},{1,0},{2,3},{3,2},{4,5},{5,4},{6,7},{7,6},{8,9},{9,8},{10,11... | collective-permute-start | bytes 1179656 | tf_op jit(solution)/shard_map/ppermute | solution.py:21
  3.8 1.3 %collective-permute-start = (bf16[3,256,256]{2,1,0:T(8,128)(2,1)S(1)}, bf16[3,256,256]{2,1,0:T(8,128)(2,1)S(1)}, u32[]{:S(2)}, u32[]{:S(2)}) collective-permute-start(bf16[3,256,256]{2,1,0:T(8,128)(2,1)S(1)} %get-tuple-element.18), channel_id=1, source_target_pairs={{0,127},{1,2},{2,1},{3,4},{4,3},{5,6},{6,5},{7,8},{8,7},{9,10},{10... | collective-permute-start | bytes 1179656 | tf_op jit(solution)/shard_map/ppermute | solution.py:21
  5.1 0.0 copy-start.5
  5.1 2.1 %mirror_rows.1 = (f32[32,3,4,128]{3,2,1,0:T(4,128)}, f32[12,128]{1,0:T(8,128)S(1)}, f32[1,128]{1,0:T(1,128)S(1)}) custom-call(f32[3]{0:T(128)S(1)} %copy-done.8, s32[1,448]{1,0:T(1,128)S(1)} %bitcast.10, f32[1,448]{1,0:T(1,128)S(1)} %bitcast.11, bf16[384,3584]{1,0:T(8,128)(2,1)S(1)} %get-tuple-element.14.picks_ref, ...), custom_call_target="tpu_custom_call" | custom-call | tf_op jit(solution)/shard_map/mirror_rows/pallas_call | solution.py:382
  7.2 11.1 %all-to-all-start = ((f32[32,3,4,128]{3,2,1,0:T(4,128)}), f32[32,3,4,128]{3,2,1,0:T(4,128)S(1)}, u32[]{:S(2)}, u32[]{:S(2)}) async-start(f32[32,3,4,128]{3,2,1,0:T(4,128)} %get-tuple-element.21), calls=%async_computation | async-start | bytes 393216 | tf_op jit(solution)/shard_map/all_to_all | solution.py:400
  18.3 0.0 copy-start.2
  18.3 0.0 copy-start.3
  18.3 0.0 copy-start.4
  18.4 0.0 collective-permute-done.1.refs_2_
  18.4 2.5 %pick_own.1.refs_3_ = bf16[3,256,1024]{2,1,0:T(8,128)(2,1)S(1)} custom-call(s32[3,4,256]{2,1,0:T(4,128)S(1)} %bitcast.7, bf16[3,1024,256]{2,1,0:T(8,128)(2,1)S(1)} %copy-done, bf16[3,256,256]{2,1,0:T(8,128)(2,1)S(1)} %collective-permute-done.1.refs_2_), custom_call_target="tpu_custom_call" | custom-call | tf_op jit(solution)/shard_map/pick_own/pallas_call | solution.py:402
  20.9 0.0 copy-start.1
  21.0 2.3 %sense_rest.1 = (f32[2,256]{1,0:T(2,128)S(1)}, f32[4,128]{1,0:T(4,128)S(1)}) custom-call(s32[3,4,256]{2,1,0:T(4,128)S(1)} %bitcast.8, bf16[3,256,256]{2,1,0:T(8,128)(2,1)S(1)} %collective-permute-done.refs_1_, bf16[3,4,256,256]{3,2,1,0:T(8,128)(2,1)S(1)} %copy-done.2, bf16[3,256,1024]{2,1,0:T(8,128)(2,1)S(1)} %pick_own.1.refs_3_, f32[256,256]{1,0:T(8,128)S(1)} %copy-done.4, ...), custom_call_target="tpu_custom_call" | custom-call | tf_op jit(solution)/shard_map/sense_rest/pallas_call | solution.py:409
  23.3 3.4 %all-to-all-done.refs_1_ = f32[32,3,4,128]{3,2,1,0:T(4,128)S(1)} async-done(((f32[32,3,4,128]{3,2,1,0:T(4,128)}), f32[32,3,4,128]{3,2,1,0:T(4,128)S(1)}, u32[]{:S(2)}, u32[]{:S(2)}) %all-to-all-start) | async-done | bytes 196640 | tf_op jit(solution)/shard_map/all_to_all | solution.py:400
  26.7 0.1 pack.1
  26.8 11.3 %all_to_all.10.refs_0_ = bf16[32,8,128]{2,1,0:T(8,128)(2,1)S(1)} all-to-all(bf16[32,8,128]{2,1,0:T(8,128)(2,1)S(1)} %pack.1), channel_id=1, replica_groups=mesh['grp'=4,'tile'=32] {'tile'}, dimensions={0} | all-to-all | bytes 131072 | tf_op jit(solution)/shard_map/all_to_all | solution.py:429
  38.1 0.6 %reconstruct.1.refs_0_ = f32[8,128]{1,0:T(8,128)S(1)} custom-call(bf16[32,8,128]{2,1,0:T(8,128)(2,1)S(1)} %all_to_all.10.refs_0_, bf16[3584,128]{1,0:T(8,128)(2,1)S(1)} %bitcast.6, s32[32,128]{1,0:T(8,128)S(1)} %get-tuple-element.23.refs_2_), custom_call_target="tpu_custom_call" | custom-call | tf_op jit(solution)/shard_map/reconstruct/pallas_call | solution.py:430
  38.7 0.5 %collective-permute-start.4 = (f32[8,128]{1,0:T(8,128)S(1)}, f32[8,128]{1,0:T(8,128)S(1)}, u32[]{:S(2)}, u32[]{:S(2)}) collective-permute-start(f32[8,128]{1,0:T(8,128)S(1)} %reconstruct.1.refs_0_), channel_id=1, source_target_pairs={{0,96},{32,0},{64,32},{96,64},{1,97},{33,1},{65,33},{97,65},{2,98}... | collective-permute-start | bytes 12296 | tf_op jit(solution)/shard_map/ppermute | solution.py:440
  39.2 0.1 collective-permute-start.3
  39.3 1.0 %collective-permute-start.2 = (f32[8,128]{1,0:T(8,128)S(1)}, f32[8,128]{1,0:T(8,128)S(1)}, u32[]{:S(2)}, u32[]{:S(2)}) collective-permute-start(f32[8,128]{1,0:T(8,128)S(1)} %reconstruct.1.refs_0_), channel_id=1, source_target_pairs={{0,32},{32,64},{64,96},{96,0},{1,33},{33,65},{65,97},{97,1},{2,34}... | collective-permute-start | bytes 12296 | tf_op jit(solution)/shard_map/ppermute | solution.py:440
  40.3 1.0 %collective-permute-done.4.refs_3_ = f32[8,128]{1,0:T(8,128)S(1)} collective-permute-done((f32[8,128]{1,0:T(8,128)S(1)}, f32[8,128]{1,0:T(8,128)S(1)}, u32[]{:S(2)}, u32[]{:S(2)}) %collective-permute-start.4) | collective-permute-done | bytes 4128 | tf_op jit(solution)/shard_map/ppermute | solution.py:440
  41.2 2.0 %collective-permute-done.3.refs_2_ = f32[8,128]{1,0:T(8,128)S(1)} collective-permute-done((f32[8,128]{1,0:T(8,128)S(1)}, f32[8,128]{1,0:T(8,128)S(1)}, u32[]{:S(2)}, u32[]{:S(2)}) %collective-permute-start.3) | collective-permute-done | bytes 4128 | tf_op jit(solution)/shard_map/ppermute | solution.py:440
  43.2 0.4 collective-permute-done.2.refs_1_
  43.6 0.7 %settle.1 = (f32[2,256]{1,0:T(2,128)}, f32[448]{0:T(512)}) custom-call(f32[8,128]{1,0:T(8,128)S(1)} %reconstruct.1.refs_0_, f32[8,128]{1,0:T(8,128)S(1)} %collective-permute-done.2.refs_1_, f32[8,128]{1,0:T(8,128)S(1)} %collective-permute-done.3.refs_2_, f32[8,128]{1,0:T(8,128)S(1)} %collective-permute-done.4.refs_3_, ...), custom_call_target="tpu_custom_call" | custom-call | tf_op jit(solution)/shard_map/settle/pallas_call | solution.py:441
  (14 shorter events, 0.0 us)
Async XLA Ops:
  0.6 4.4 %copy-start.6 = (s32[448]{0:T(512)S(1)}, s32[448]{0:T(512)}, u32[]{:S(2)}) copy-start(s32[448]{0:T(512)} %param.17) | copy-start | bytes 5380
  0.6 4.4 %copy-start.8 = (f32[3]{0:T(128)S(1)}, f32[3]{0:T(128)}, u32[]{:S(2)}) copy-start(f32[3]{0:T(128)} %gain_ref.1) | copy-start | bytes 40
  0.7 4.4 %copy-start.7 = (f32[448]{0:T(512)S(1)}, f32[448]{0:T(512)}, u32[]{:S(2)}) copy-start(f32[448]{0:T(512)} %param.16) | copy-start | bytes 5380
  2.3 16.0 %collective-permute-start.1 = (bf16[3,256,256]{2,1,0:T(8,128)(2,1)S(1)}, bf16[3,256,256]{2,1,0:T(8,128)(2,1)S(1)}, u32[]{:S(2)}, u32[]{:S(2)}) collective-permute-start(bf16[3,256,256]{2,1,0:T(8,128)(2,1)S(1)} %get-tuple-element.19), channel_id=1, source_target_pairs={{0,1},{1,0},{2,3},{3,2},{4,5},{5,4},{6,7},{7,6},{8,9},{9,8},{10,11... | collective-permute-start | bytes 1179656 | tf_op jit(solution)/shard_map/ppermute | solution.py:21
  3.8 17.2 %collective-permute-start = (bf16[3,256,256]{2,1,0:T(8,128)(2,1)S(1)}, bf16[3,256,256]{2,1,0:T(8,128)(2,1)S(1)}, u32[]{:S(2)}, u32[]{:S(2)}) collective-permute-start(bf16[3,256,256]{2,1,0:T(8,128)(2,1)S(1)} %get-tuple-element.18), channel_id=1, source_target_pairs={{0,127},{1,2},{2,1},{3,4},{4,3},{5,6},{6,5},{7,8},{8,7},{9,10},{10... | collective-permute-start | bytes 1179656 | tf_op jit(solution)/shard_map/ppermute | solution.py:21
  5.1 13.3 %copy-start = (bf16[3,1024,256]{2,1,0:T(8,128)(2,1)S(1)}, bf16[3,1024,256]{2,1,0:T(8,128)(2,1)}, u32[]{:S(2)}) copy-start(bf16[3,1024,256]{2,1,0:T(8,128)(2,1)} %refs_1_.1) | copy-start | bytes 4718596
  5.1 13.3 %copy-start.5 = (s32[256,3,4]{0,2,1:T(4,128)S(1)}, s32[256,3,4]{0,2,1:T(4,128)}, u32[]{:S(2)}) copy-start(s32[256,3,4]{0,2,1:T(4,128)} %param.12) | copy-start | bytes 36868
  7.2 19.5 %all-to-all-start = ((f32[32,3,4,128]{3,2,1,0:T(4,128)}), f32[32,3,4,128]{3,2,1,0:T(4,128)S(1)}, u32[]{:S(2)}, u32[]{:S(2)}) async-start(f32[32,3,4,128]{3,2,1,0:T(4,128)} %get-tuple-element.21), calls=%async_computation | async-start | bytes 393216 | tf_op jit(solution)/shard_map/all_to_all | solution.py:400
  18.3 2.6 %copy-start.2 = (bf16[3,4,256,256]{3,2,1,0:T(8,128)(2,1)S(1)}, bf16[3,4,256,256]{3,2,1,0:T(8,128)(2,1)}, u32[]{:S(2)}) copy-start(bf16[3,4,256,256]{3,2,1,0:T(8,128)(2,1)} %refs_2_.1) | copy-start | bytes 4718596
  18.3 2.6 %copy-start.3 = (bf16[512,512]{1,0:T(8,128)(2,1)S(1)}, bf16[512,512]{1,0:T(8,128)(2,1)}, u32[]{:S(2)}) copy-start(bf16[512,512]{1,0:T(8,128)(2,1)} %constant.2.clone.refs_5_) | copy-start | bytes 1572868
  18.3 2.6 %copy-start.4 = (f32[256,256]{1,0:T(8,128)S(1)}, f32[256,256]{1,0:T(8,128)}, u32[]{:S(2)}) copy-start(f32[256,256]{1,0:T(8,128)} %refs_4_.1) | copy-start | bytes 786436
  20.9 17.1 %copy-start.1 = (bf16[28,4,16,2,128]{4,3,2,1,0:T(2,128)(2,1)S(1)}, bf16[28,4,16,2,128]{4,3,2,1,0:T(2,128)(2,1)}, u32[]{:S(2)}) copy-start(bf16[28,4,16,2,128]{4,3,2,1,0:T(2,128)(2,1)} %param.14) | copy-start | bytes 2752516
  38.7 2.5 %collective-permute-start.4 = (f32[8,128]{1,0:T(8,128)S(1)}, f32[8,128]{1,0:T(8,128)S(1)}, u32[]{:S(2)}, u32[]{:S(2)}) collective-permute-start(f32[8,128]{1,0:T(8,128)S(1)} %reconstruct.1.refs_0_), channel_id=1, source_target_pairs={{0,96},{32,0},{64,32},{96,64},{1,97},{33,1},{65,33},{97,65},{2,98}... | collective-permute-start | bytes 12296 | tf_op jit(solution)/shard_map/ppermute | solution.py:440
  39.2 4.0 %collective-permute-start.3 = (f32[8,128]{1,0:T(8,128)S(1)}, f32[8,128]{1,0:T(8,128)S(1)}, u32[]{:S(2)}, u32[]{:S(2)}) collective-permute-start(f32[8,128]{1,0:T(8,128)S(1)} %reconstruct.1.refs_0_), channel_id=1, source_target_pairs={{0,64},{32,96},{64,0},{96,32},{1,65},{33,97},{65,1},{97,33},{2,66}... | collective-permute-start | bytes 12296 | tf_op jit(solution)/shard_map/ppermute | solution.py:440
  39.3 4.3 %collective-permute-start.2 = (f32[8,128]{1,0:T(8,128)S(1)}, f32[8,128]{1,0:T(8,128)S(1)}, u32[]{:S(2)}, u32[]{:S(2)}) collective-permute-start(f32[8,128]{1,0:T(8,128)S(1)} %reconstruct.1.refs_0_), channel_id=1, source_target_pairs={{0,32},{32,64},{64,96},{96,0},{1,33},{33,65},{65,97},{97,1},{2,34}... | collective-permute-start | bytes 12296 | tf_op jit(solution)/shard_map/ppermute | solution.py:440
